TPU v7x, 256 devices: a whole 4x4x8 slice. The times are simulated.
256 devices in a mesh: pipe: 8 (over z), dp: 4 (over y), expert: 8 (over x, core).
Axes of the slice: x: 4, y: 4, z: 8, core: 2. Of those that a mesh axis runs over, the one named last changes fastest.
Arguments:
- tokens: bfloat16 [4096, 4096], P(('dp', 'expert'), 'pipe'), may hold values from -6 to 6
- routes: int32 [4096, 6], P(('dp', 'expert')), may hold values from 0 to 31, all different within a row; in each aligned block of 128 rows (0 to 127, 128 to 255, ...) at most 32 rows name the same one
- gates: float32 [4096, 6], P(('dp', 'expert')), may hold values from 0.1 to 0.5
- w_gate: bfloat16 [32, 4096, 1024], P(('dp', 'expert'), 'pipe'), may hold values from -0.09375 to 0.09375
- w_up: bfloat16 [32, 4096, 1024], P(('dp', 'expert'), 'pipe'), may hold values from -0.09375 to 0.09375
- w_down: bfloat16 [32, 1024, 4096], P(('dp', 'expert'), None, 'pipe'), may hold values from -0.1875 to 0.1875
- grad_out: bfloat16 [4096, 4096], P(('dp', 'expert'), 'pipe'), may hold values from -6 to 6
Outputs:
- mixed: bfloat16 [4096, 4096], P(('dp', 'expert'), 'pipe')
- grad_tokens: bfloat16 [4096, 4096], P(('dp', 'expert'), 'pipe')
- grad_gate: bfloat16 [32, 4096, 1024], P(('dp', 'expert'), 'pipe')
- grad_up: bfloat16 [32, 4096, 1024], P(('dp', 'expert'), 'pipe')
- grad_down: bfloat16 [32, 1024, 4096], P(('dp', 'expert'), None, 'pipe')
Inputs may be any that keep to these rules, and one draw needn't show every extreme that they name: `routes`: each row names 6 different experts; in each aligned block of 128 rows no expert is named by more than 32 rows, a bound that some block reaches.
All inputs are finite; a program needn't handle non-finite values.
Results may differ from a plain program's by a relative error of at most 0.0065.
Values may be sent and summed in bfloat16 or wider, within the bound.
A program may use at most 128 MiB of HBM per device.

v0:
```python
import jax
import jax.numpy as jnp
from jax import lax
from jax.sharding import PartitionSpec as P

CAP = 32


def slot_layout(routes, num_experts):
    tok_count, top_count = routes.shape
    chosen = routes.reshape(tok_count * top_count)
    expert_ids = jnp.arange(num_experts, dtype=jnp.int32)
    onehot = (chosen[:, None] == expert_ids[None, :]).astype(jnp.int32)
    earlier = jnp.cumsum(onehot, axis=0) - onehot
    position = jnp.sum(earlier * onehot, axis=1)
    target = chosen * CAP + position
    slot_ids = jnp.arange(num_experts * CAP, dtype=jnp.int32)
    placed = slot_ids[:, None] == target[None, :]
    return placed.reshape(num_experts * CAP, tok_count, top_count)


def local(tokens, routes, gates, w_gate, w_up, w_down, grad_out):
    groups = lax.axis_size(("dp", "expert"))
    local_experts = w_gate.shape[0]
    num_experts = local_experts * groups
    slice_width = tokens.shape[1]
    placed = slot_layout(routes, num_experts)
    dispatch = jnp.sum(placed.astype(jnp.int32), axis=2).astype(jnp.bfloat16)
    mixing = jnp.sum(jnp.where(placed, gates[None, :, :], 0.0), axis=2)
    outbound = jnp.dot(dispatch, tokens, preferred_element_type=jnp.float32).astype(jnp.bfloat16)
    outbound = outbound.reshape(num_experts, CAP, slice_width)
    scaled_out = jnp.dot(
        mixing, grad_out.astype(jnp.float32), precision=lax.Precision.HIGHEST
    ).astype(jnp.bfloat16)
    scaled_out = scaled_out.reshape(num_experts, CAP, slice_width)
    arrived, arrived_grad = (
        lax.all_to_all(outbound, ("dp", "expert"), split_axis=0, concat_axis=0, tiled=True),
        lax.all_to_all(scaled_out, ("dp", "expert"), split_axis=0, concat_axis=0, tiled=True),
    )
    expert_rows = arrived.reshape(groups, local_experts, CAP, slice_width)
    scaled = arrived_grad.reshape(groups, local_experts, CAP, slice_width)
    gate_part = jnp.einsum(
        "sjcd,jdf->sjcf", expert_rows, w_gate, preferred_element_type=jnp.float32
    )
    up_part = jnp.einsum("sjcd,jdf->sjcf", expert_rows, w_up, preferred_element_type=jnp.float32)
    gate_share, up_share = (
        lax.psum_scatter(gate_part, "pipe", scatter_dimension=3, tiled=True),
        lax.psum_scatter(up_part, "pipe", scatter_dimension=3, tiled=True),
    )
    hidden_share = (jax.nn.silu(gate_share) * up_share).astype(jnp.bfloat16)
    hidden = lax.all_gather(hidden_share, "pipe", axis=3, tiled=True)
    expert_out = jnp.einsum(
        "sjcf,jfd->sjcd", hidden, w_down, preferred_element_type=jnp.float32
    ).astype(jnp.bfloat16)
    returned = lax.all_to_all(
        expert_out.reshape(num_experts, CAP, slice_width),
        ("dp", "expert"),
        split_axis=0,
        concat_axis=0,
        tiled=True,
    )
    returned_rows = returned.reshape(num_experts * CAP, slice_width).astype(jnp.float32)
    mixed = jnp.dot(mixing.T, returned_rows, precision=lax.Precision.HIGHEST).astype(jnp.bfloat16)
    d_hidden_part = jnp.einsum("sjcd,jfd->sjcf", scaled, w_down, preferred_element_type=jnp.float32)
    d_hidden = lax.psum_scatter(d_hidden_part, "pipe", scatter_dimension=3, tiled=True)
    sig_gate = jax.nn.sigmoid(gate_share)
    d_gate_share = (d_hidden * up_share * sig_gate * (1.0 + gate_share * (1.0 - sig_gate))).astype(
        jnp.bfloat16
    )
    d_up_share = (d_hidden * gate_share * sig_gate).astype(jnp.bfloat16)
    d_gate, d_up = (
        lax.all_gather(d_gate_share, "pipe", axis=3, tiled=True),
        lax.all_gather(d_up_share, "pipe", axis=3, tiled=True),
    )
    d_rows = (
        jnp.einsum("sjcf,jdf->sjcd", d_gate, w_gate, preferred_element_type=jnp.float32)
        + jnp.einsum("sjcf,jdf->sjcd", d_up, w_up, preferred_element_type=jnp.float32)
    ).astype(jnp.bfloat16)
    back_rows = lax.all_to_all(
        d_rows.reshape(num_experts, CAP, slice_width),
        ("dp", "expert"),
        split_axis=0,
        concat_axis=0,
        tiled=True,
    )
    grad_tokens = jnp.dot(
        dispatch.T,
        back_rows.reshape(num_experts * CAP, slice_width),
        preferred_element_type=jnp.float32,
    ).astype(jnp.bfloat16)
    grad_gate = jnp.einsum(
        "sjcd,sjcf->jdf", expert_rows, d_gate, preferred_element_type=jnp.float32
    ).astype(jnp.bfloat16)
    grad_up = jnp.einsum(
        "sjcd,sjcf->jdf", expert_rows, d_up, preferred_element_type=jnp.float32
    ).astype(jnp.bfloat16)
    grad_down = jnp.einsum(
        "sjcf,sjcd->jfd", hidden, scaled, preferred_element_type=jnp.float32
    ).astype(jnp.bfloat16)
    return (mixed, grad_tokens, grad_gate, grad_up, grad_down)


def solution(mesh):
    placed = (
        P(("dp", "expert"), "pipe"),
        P(("dp", "expert"), None),
        P(("dp", "expert"), None),
        P(("dp", "expert"), "pipe", None),
        P(("dp", "expert"), "pipe", None),
        P(("dp", "expert"), None, "pipe"),
        P(("dp", "expert"), "pipe"),
    )
    return jax.shard_map(
        local,
        mesh=mesh,
        in_specs=placed,
        out_specs=(
            P(("dp", "expert"), "pipe"),
            P(("dp", "expert"), "pipe"),
            P(("dp", "expert"), "pipe", None),
            P(("dp", "expert"), "pipe", None),
            P(("dp", "expert"), None, "pipe"),
        ),
        check_vma=False,
    )
```

profile of v0, /device:TPU:1, one launch (start us, length us, event | category | flops | bytes accessed | tf_op | source)
XLA Modules:
  0.0 395.7 jit_solution(5158708211324095132)
XLA Ops:
  7.2 0.0 copy-start
  7.2 0.0 reduce-scatter.6.cloned.1.call-start
  7.2 0.9 copy.38
  8.1 0.1 eq.44
  8.2 0.1 eq.40
  8.4 1.7 reduce-window.6
  10.1 0.3 slice_reduce_fusion
  10.4 0.1 fusion.42
  10.5 0.1 reduce_sum.30
  10.7 0.1 copy.41
  10.7 0.7 multiply_add_fusion
  11.5 0.0 copy-start.4
  11.5 0.4 convert_reduce_fusion
  11.8 1.3 convolution_convert_fusion
  13.2 25.6 %all_to_all.20 = bf16[32,32,512]{2,1,0:T(8,128)(2,1)S(1)} all-to-all(bf16[32,32,512]{2,1,0:T(8,128)(2,1)S(1)} %bitcast.121), channel_id=1, replica_groups=mesh['pipe'=8,'dp'=4,'expert'=8] {'dp','expert'}, dimensions={0} | all-to-all | bytes 2097152 | tf_op jit(solution)/shard_map/all_to_all | solution.py:37
  38.7 0.0 copy-done.4
  38.7 3.2 convolution_bitcast_fusion.1
  41.9 0.0 reduce-scatter.6.cloned.1.call-update
  42.0 0.0 reduce-scatter.4.cloned.1.call-start
  42.0 4.4 %convolution_bitcast_fusion.2 = f32[32,1,32,1024]{3,2,0,1:T(8,128)} fusion(bf16[32,32,512]{2,1,0:T(8,128)(2,1)S(1)} %all_to_all.20, bf16[1,512,1024]{2,1,0:T(8,128)(2,1)} %param.10), kind=kOutput, calls=%fused_computation.5 | convolution fusion | flops 1073741824 | bytes 6291456 | tf_op jit(solution)/shard_map/sjcd,jdf->sjcf/dot_general | solution.py:42
  46.5 0.0 copy-start.6
  46.5 0.0 copy-start.5
  46.5 0.0 reduce-scatter.4.cloned.1.call-update
  46.5 0.0 reduce-scatter.8.cloned.1.call-start
  46.5 0.6 copy-done.6
  47.1 0.4 select_reduce_fusion
  47.5 0.0 copy-done.5
  47.5 1.0 convolution_convert_fusion.1
  48.5 20.7 %all_to_all.21 = bf16[32,32,512]{2,1,0:T(8,128)(2,1)S(1)} all-to-all(bf16[32,32,512]{2,1,0:T(8,128)(2,1)S(1)} %bitcast.122), channel_id=1, replica_groups=mesh['pipe'=8,'dp'=4,'expert'=8] {'dp','expert'}, dimensions={0} | all-to-all | bytes 2097152 | tf_op jit(solution)/shard_map/all_to_all | solution.py:38
  69.2 0.0 copy-start.1
  69.2 1.0 copy-done.1
  70.2 0.0 copy-done
  70.2 3.2 convolution_bitcast_fusion
  73.4 0.0 reduce-scatter.8.cloned.1.call-update
  73.4 0.0 all-gather.4.cloned.1.call-start
  73.5 23.0 %reduce-scatter.6.cloned.1.call-done = f32[32,1,32,128]{3,2,0,1:T(8,128)} async-done(((f32[32,1,32,1024]{3,2,0,1:T(8,128)}), f32[32,1,32,128]{3,2,0,1:T(8,128)}) %reduce-scatter.6.cloned.1.call-update) | async-done | bytes 524304 | tf_op jit(solution)/shard_map/reduce_scatter | solution.py:48
  96.4 56.5 %reduce-scatter.4.cloned.1.call-done = f32[32,1,32,128]{3,2,0,1:T(8,128)} async-done(((f32[32,1,32,1024]{3,2,0,1:T(8,128)}), f32[32,1,32,128]{3,2,0,1:T(8,128)}) %reduce-scatter.4.cloned.1.call-update) | async-done | bytes 524304 | tf_op jit(solution)/shard_map/reduce_scatter | solution.py:47
  153.0 56.5 %reduce-scatter.8.cloned.1.call-done = f32[32,1,32,128]{3,2,0,1:T(8,128)} async-done(((f32[32,1,32,1024]{3,2,0,1:T(8,128)}), f32[32,1,32,128]{3,2,0,1:T(8,128)}) %reduce-scatter.8.cloned.1.call-update) | async-done | bytes 524304 | tf_op jit(solution)/shard_map/reduce_scatter | solution.py:65
  209.5 2.5 multiply_convert_fusion.1
  212.0 0.0 all-gather.4.cloned.1.call-update
  212.0 0.0 all-gather.8.cloned.1.call-start
  212.1 0.5 all-gather.8.cloned.1.call-update
  212.6 0.0 all-gather.6.cloned.1.call-start
  212.7 0.5 all-gather.6.cloned.1.call-update
  213.2 41.1 %all-gather.4.cloned.1.call-done = bf16[32,1,32,1024]{3,2,0,1:T(8,128)(2,1)} async-done(((bf16[32,1,32,128]{3,2,0,1:T(8,128)(2,1)}), bf16[32,1,32,1024]{3,2,0,1:T(8,128)(2,1)}) %all-gather.4.cloned.1.call-update) | async-done | bytes 2097168 | tf_op jit(solution)/shard_map/all_gather | solution.py:51
  254.3 3.8 fusion.20
  258.1 11.2 %all-to-all-start.1 = ((bf16[32,32,512]{2,1,0:T(8,128)(2,1)}), bf16[32,32,512]{2,1,0:T(8,128)(2,1)}, u32[]{:S(2)}, u32[]{:S(2)}) async-start(bf16[32,32,512]{2,1,0:T(8,128)(2,1)} %fusion.20), calls=%async_computation.3 | async-start | bytes 2097152 | tf_op jit(solution)/shard_map/all_to_all | solution.py:55
  269.4 33.0 %all-gather.8.cloned.1.call-done = bf16[32,1,32,1024]{3,2,0,1:T(8,128)(2,1)} async-done(((bf16[32,1,32,128]{3,2,0,1:T(8,128)(2,1)}), bf16[32,1,32,1024]{3,2,0,1:T(8,128)(2,1)}) %all-gather.8.cloned.1.call-update) | async-done | bytes 2097168 | tf_op jit(solution)/shard_map/all_gather | solution.py:73
  302.4 0.0 copy-start.2
  302.4 0.0 copy-start.7
  302.4 4.6 %fusion.2 = f32[32,32,512]{2,1,0:T(8,128)} fusion(bf16[32,1,32,1024]{3,2,0,1:T(8,128)(2,1)} %all-gather.8.cloned.1.call-done, bf16[1,512,1024]{2,1,0:T(8,128)(2,1)} %param.11), kind=kOutput, calls=%fused_computation.11 | convolution fusion | flops 1073741824 | bytes 5242880 | tf_op jit(solution)/shard_map/sjcf,jdf->sjcd/dot_general | solution.py:77
  307.0 0.0 copy-done.2
  307.0 0.0 copy-done.7
  307.0 2.3 fusion.29
  309.3 41.7 %all-gather.6.cloned.1.call-done = bf16[32,1,32,1024]{3,2,0,1:T(8,128)(2,1)} async-done(((bf16[32,1,32,128]{3,2,0,1:T(8,128)(2,1)}), bf16[32,1,32,1024]{3,2,0,1:T(8,128)(2,1)}) %all-gather.6.cloned.1.call-update) | async-done | bytes 2097168 | tf_op jit(solution)/shard_map/all_gather | solution.py:72
  351.0 5.0 %add_convert_fusion = bf16[32,32,512]{2,1,0:T(8,128)(2,1)} fusion(f32[32,32,512]{2,1,0:T(8,128)} %fusion.2, bf16[32,1,32,1024]{3,2,0,1:T(8,128)(2,1)} %all-gather.6.cloned.1.call-done, bf16[1,512,1024]{2,1,0:T(8,128)(2,1)} %param.10), kind=kOutput, calls=%fused_computation.21 | convolution fusion | flops 1074790400 | bytes 6291456 | tf_op jit(solution)/shard_map/sjcf,jdf->sjcd/dot_general | solution.py:76
  355.9 0.0 copy-done.3
  355.9 2.2 fusion.26
  358.2 0.0 all-to-all-done.1
  358.2 11.2 %all-to-all-start.3 = ((bf16[32,32,512]{2,1,0:T(8,128)(2,1)}), bf16[32,32,512]{2,1,0:T(8,128)(2,1)}, u32[]{:S(2)}, u32[]{:S(2)}) async-start(bf16[32,32,512]{2,1,0:T(8,128)(2,1)} %add_convert_fusion), calls=%async_computation.6 | async-start | bytes 2097152 | tf_op jit(solution)/shard_map/all_to_all | solution.py:79
  369.4 3.8 fusion.23
  373.3 2.6 convolution_convert_fusion.3
  375.8 10.8 %all-to-all-done.3 = bf16[32,32,512]{2,1,0:T(8,128)(2,1)} async-done(((bf16[32,32,512]{2,1,0:T(8,128)(2,1)}), bf16[32,32,512]{2,1,0:T(8,128)(2,1)}, u32[]{:S(2)}, u32[]{:S(2)}) %all-to-all-start.3) | async-done | bytes 1048608 | tf_op jit(solution)/shard_map/all_to_all | solution.py:79
  386.7 2.2 convolution_convert_fusion.2
  (3 shorter events, 0.0 us)
Async XLA Ops:
  7.2 63.0 %copy-start = (bf16[1,1024,512]{2,1,0:T(8,128)(2,1)S(1)}, bf16[1,1024,512]{2,1,0:T(8,128)(2,1)}, u32[]{:S(2)}) copy-start(bf16[1,1024,512]{2,1,0:T(8,128)(2,1)} %param.12) | copy-start | bytes 3145732
  7.2 89.3 %reduce-scatter.6.cloned.1.call-start = ((), (), s32[]{:S(2)}) async-start(), calls=%async_computation.8 | async-start | bytes 4718592 | tf_op jit(solution)/shard_map/reduce_scatter | solution.py:48
  11.5 27.3 %copy-start.4 = (bf16[1,512,1024]{2,1,0:T(8,128)(2,1)S(1)}, bf16[1,512,1024]{2,1,0:T(8,128)(2,1)}, u32[]{:S(2)}) copy-start(bf16[1,512,1024]{2,1,0:T(8,128)(2,1)} %param.11) | copy-start | bytes 3145732
  42.0 111.0 %reduce-scatter.4.cloned.1.call-start = ((), (), s32[]{:S(2)}) async-start(), calls=%async_computation.7 | async-start | bytes 4718592 | tf_op jit(solution)/shard_map/reduce_scatter | solution.py:47
  46.5 0.7 copy-start.6
  46.5 1.1 copy-start.5
  46.5 163.0 %reduce-scatter.8.cloned.1.call-start = ((), (), s32[]{:S(2)}) async-start(), calls=%async_computation.10 | async-start | bytes 4718592 | tf_op jit(solution)/shard_map/reduce_scatter | solution.py:65
  69.2 1.0 copy-start.1
  73.4 180.9 %all-gather.4.cloned.1.call-start = ((), (), s32[]{:S(2)}) async-start(), calls=%async_computation.9 | async-start | bytes 2359296 | tf_op jit(solution)/shard_map/all_gather | solution.py:51
  212.0 90.3 %all-gather.8.cloned.1.call-start = ((), (), s32[]{:S(2)}) async-start(), calls=%async_computation.12 | async-start | bytes 2359296 | tf_op jit(solution)/shard_map/all_gather | solution.py:73
  212.6 138.4 %all-gather.6.cloned.1.call-start = ((), (), s32[]{:S(2)}) async-start(), calls=%async_computation.11 | async-start | bytes 2359296 | tf_op jit(solution)/shard_map/all_gather | solution.py:72
  258.1 100.1 %all-to-all-start.1 = ((bf16[32,32,512]{2,1,0:T(8,128)(2,1)}), bf16[32,32,512]{2,1,0:T(8,128)(2,1)}, u32[]{:S(2)}, u32[]{:S(2)}) async-start(bf16[32,32,512]{2,1,0:T(8,128)(2,1)} %fusion.20), calls=%async_computation.3 | async-start | bytes 2097152 | tf_op jit(solution)/shard_map/all_to_all | solution.py:55
  302.4 4.6 %copy-start.2 = (bf16[32,32,512]{2,1,0:T(8,128)(2,1)S(1)}, bf16[32,32,512]{2,1,0:T(8,128)(2,1)}, u32[]{:S(2)}) copy-start(bf16[32,32,512]{2,1,0:T(8,128)(2,1)} %copy-done.1) | copy-start | bytes 3145732
  302.4 4.6 %copy-start.7 = (bf16[32,1,32,1024]{3,2,0,1:T(8,128)(2,1)S(1)}, bf16[32,1,32,1024]{3,2,0,1:T(8,128)(2,1)}, u32[]{:S(2)}) copy-start(bf16[32,1,32,1024]{3,2,0,1:T(8,128)(2,1)} %all-gather.4.cloned.1.call-done) | copy-start | bytes 6291460
  351.0 5.0 %copy-start.3 = (bf16[32,1,32,1024]{3,2,0,1:T(8,128)(2,1)S(1)}, bf16[32,1,32,1024]{3,2,0,1:T(8,128)(2,1)}, u32[]{:S(2)}) copy-start(bf16[32,1,32,1024]{3,2,0,1:T(8,128)(2,1)} %all-gather.8.cloned.1.call-done) | copy-start | bytes 6291460
  358.2 28.5 %all-to-all-start.3 = ((bf16[32,32,512]{2,1,0:T(8,128)(2,1)}), bf16[32,32,512]{2,1,0:T(8,128)(2,1)}, u32[]{:S(2)}, u32[]{:S(2)}) async-start(bf16[32,32,512]{2,1,0:T(8,128)(2,1)} %add_convert_fusion), calls=%async_computation.6 | async-start | bytes 2097152 | tf_op jit(solution)/shard_map/all_to_all | solution.py:79
Sparse Core Ops, SparseCore 0:
  42.1 54.3 reduce-scatter.5
  99.0 53.9 reduce-scatter.3
  155.5 53.9 reduce-scatter.7
  212.1 42.1 all-gather.3
  255.9 46.4 all-gather.7
  304.5 46.4 all-gather.5
where the time goes:
time: 396 us
  waiting for transfers between devices  264 us (67%)
  blocking collectives  46.3 us (12%)
  matrix products  39.7 us (10%)
  starting transfers between devices  22.7 us (6%)
  between operations  14.2 us (4%)
  other arithmetic  5.89 us (1%)
    reduce_scatter x1, waiting for transfers between devices, local(): lax.psum_scatter(d_hidden_part, 'pipe', scatter_dimension=3, tiled=True)  56.5 us
    reduce_scatter x1, waiting for transfers between devices, local(): lax.psum_scatter(gate_part, 'pipe', scatter_dimension=3, tiled=True)  56.5 us
    all_gather x1, waiting for transfers between devices, local(): lax.all_gather(d_gate_share, 'pipe', axis=3, tiled=True)  41.7 us
    all_gather x1, waiting for transfers between devices, local(): hidden = lax.all_gather(hidden_share, 'pipe', axis=3, tiled=True)  41.1 us
    all_gather x1, waiting for transfers between devices, local(): lax.all_gather(d_up_share, 'pipe', axis=3, tiled=True)  33 us
    all_to_all x1, blocking collectives, local(): lax.all_to_all(outbound, ('dp', 'expert'), split_axis=0, concat_axis=0, t...  25.6 us
    reduce_scatter x1, waiting for transfers between devices, local(): lax.psum_scatter(up_part, 'pipe', scatter_dimension=3, tiled=True)  23 us
    all_to_all x1, blocking collectives, local(): lax.all_to_all(scaled_out, ('dp', 'expert'), split_axis=0, concat_axis=0,...  20.7 us
  transfers between devices with their start and end apart: 8, of which 7 were waited for; matrix products, arithmetic and copies ran while one was open for 8% of the time, Pallas kernels for 0%

commit v1 on v0

v1 whole, which is shorter than its diff:
```python
import functools

import jax
import jax.numpy as jnp
from jax import lax
from jax.experimental import pallas as pl
from jax.experimental.pallas import tpu as pltpu
from jax.sharding import PartitionSpec as P

CAP = 32
MESH = pl.DeviceIdType.MESH
F32 = jnp.float32
BF16 = jnp.bfloat16
NN = (((1,), (0,)), ((), ()))
NT = (((1,), (1,)), ((), ()))


def dot(a, b, dims=NN):
    return lax.dot_general(a, b, dims, preferred_element_type=F32)


def chunk_order(dp):
    return {4: (0, 2, 1, 3), 2: (0, 1), 1: (0,)}[dp]


def kernel(
    dp, ex, pipe,
    routes_ref, gates_ref, tok_ref, go_ref, wg_hbm, wu_hbm, wd_hbm,
    mixed_ref, gtok_ref, gg_hbm, gu_hbm, gd_hbm,
    wg, wu, wd, onehot, mixw, onehot_t, mix_hi, mix_lo,
    out_x, out_g, rows_x, rows_g, part, ring_in, ring_out, full,
    acc_g, acc_u, acc_d, grad_g, grad_u, grad_d, eo_buf, dr_buf, ret_e, ret_d,
    w_sem, self_sem, send_a2a, recv_x, recv_g, send_ret, recv_ret,
    ring_send, ring_recv, full_send, full_recv, store_sem,
):
    p = lax.axis_index("pipe")
    y = lax.axis_index("dp")
    e = lax.axis_index("expert")
    me = y * ex + e
    groups = dp * ex
    ff = wg.shape[1]
    width = wg.shape[0]
    rows = ex * CAP
    fw = ff // pipe
    rel = chunk_order(dp)
    nxt = lax.rem(p + 1, pipe)
    prv = lax.rem(p + pipe - 1, pipe)
    half = pipe // 2

    loads = [
        pltpu.make_async_copy(src, dst, w_sem.at[i])
        for i, (src, dst) in enumerate(((wg_hbm, wg), (wu_hbm, wu), (wd_hbm, wd)))
    ]
    for load in loads:
        load.start()

    barrier = pltpu.get_barrier_semaphore()
    for r in range(dp):
        for k in range(ex):
            if r == 0 and k == 0:
                continue
            pl.semaphore_signal(
                barrier, inc=1, device_id_type=MESH,
                device_id={"dp": lax.rem(y + r, dp), "expert": lax.rem(e + k, ex)},
            )
    for other in (prv, nxt):
        pl.semaphore_signal(barrier, inc=1, device_id={"pipe": other}, device_id_type=MESH)

    toks = tok_ref.shape[0]
    eid = lax.broadcasted_iota(jnp.int32, (groups, toks), 0)
    member = jnp.zeros((groups, toks), F32)
    gate_of = jnp.zeros((groups, toks), F32)
    for k in range(routes_ref.shape[0]):
        hit = routes_ref[k : k + 1, :] == eid
        member += jnp.where(hit, 1.0, 0.0)
        gate_of += jnp.where(hit, gates_ref[k : k + 1, :], 0.0)
    before = jnp.where(
        lax.broadcasted_iota(jnp.int32, (toks, toks), 0)
        < lax.broadcasted_iota(jnp.int32, (toks, toks), 1),
        1.0, 0.0,
    ).astype(BF16)
    slot = jnp.where(member > 0.0, dot(member.astype(BF16), before), -1.0)
    slot_id = lax.broadcasted_iota(jnp.int32, (CAP, toks), 0).astype(F32)
    for i in range(groups):
        filled = slot[i : i + 1, :] == slot_id
        onehot[i * CAP : (i + 1) * CAP, :] = jnp.where(filled, 1.0, 0.0)
        mixw[i * CAP : (i + 1) * CAP, :] = jnp.where(filled, gate_of[i : i + 1, :], 0.0)
    tokens = tok_ref[...]
    grad_out = go_ref[...]
    step_rows = 256 if groups * CAP % 256 == 0 else groups * CAP
    for i in range(groups * CAP // step_rows):
        span = slice(i * step_rows, (i + 1) * step_rows)
        block = slice(i * step_rows // CAP, (i + 1) * step_rows // CAP)
        pick = onehot[span, :].astype(BF16)
        gate_row = jnp.sum(mixw[span, :], axis=1, keepdims=True)
        out_x[block] = dot(pick, tokens).astype(BF16).reshape(step_rows // CAP, CAP, width)
        out_g[block] = (
            (gate_row * dot(pick, grad_out)).astype(BF16).reshape(step_rows // CAP, CAP, width)
        )

    pl.semaphore_wait(barrier, groups - 1 + 2)

    own_copies = []
    for c in range(dp):
        to_y = lax.rem(y - rel[c] + dp, dp)
        for src, dst, recv in ((out_x, rows_x, recv_x), (out_g, rows_g, recv_g)):
            for k in range(ex):
                to_e = lax.rem(e + k, ex)
                if rel[c] == 0 and k == 0:
                    copy = pltpu.make_async_copy(
                        src.at[me], dst.at[c, e], self_sem.at[len(own_copies)]
                    )
                    copy.start()
                    own_copies.append(copy)
                    continue
                pltpu.make_async_remote_copy(
                    src_ref=src.at[to_y * ex + to_e],
                    dst_ref=dst.at[c, e],
                    send_sem=send_a2a,
                    recv_sem=recv.at[c],
                    device_id={"dp": to_y, "expert": to_e},
                    device_id_type=MESH,
                ).start()

    onehot_t[...] = onehot[...].T.astype(BF16)
    mix_t = mixw[...].T
    mix_top = mix_t.astype(BF16)
    mix_hi[...] = mix_top
    mix_lo[...] = (mix_t - mix_top.astype(F32)).astype(BF16)

    def bytes_wait(ref, sem):
        pltpu.make_async_copy(ref, ref, sem).wait()

    def arrive(c, buf, recv, own):
        if rel[c] == 0:
            own.wait()
            if ex > 1:
                view = buf.at[c, pl.ds(0, ex - 1)]
                bytes_wait(view, recv.at[c])
        else:
            bytes_wait(buf.at[c], recv.at[c])

    def x_of(c):
        return rows_x[c].reshape(rows, width)

    def g_of(c):
        return rows_g[c].reshape(rows, width)

    tile = 256

    def partial(c, q):
        a = x_of(c) if q < 2 else g_of(c)
        for n in range(ff // tile):
            cols = slice(n * tile, (n + 1) * tile)
            if q == 2:
                res = dot(a, wd[cols, :], NT)
            else:
                res = dot(a, (wg, wu)[q][:, cols])
            for i in range(tile // fw):
                part[c % 2, q, n * (tile // fw) + i] = res[:, i * fw : (i + 1) * fw]

    def hops(c, d):
        return half if (c % 2 == 0) == (d == 0) else half - 1

    def place(c, d, t):
        return t if hops(c, d) == half else half + t

    def ring_step(c, t):
        for q in range(3):
            for d in range(2):
                n = hops(c, d)
                if t >= n:
                    continue
                owner = lax.rem(p - n + t + pipe, pipe) if d == 0 else lax.rem(p + n - t, pipe)
                value = part[c % 2, q, owner]
                if t > 0:
                    got = place(c, d, t - 1)
                    bytes_wait(ring_in.at[c, q, got], ring_recv.at[c, q, got])
                    value = value + ring_in[c, q, got].astype(F32)
                m = place(c, d, t)
                ring_out[c, q, m] = value.astype(BF16)
                pltpu.make_async_remote_copy(
                    src_ref=ring_out.at[c, q, m],
                    dst_ref=ring_in.at[c, q, m],
                    send_sem=ring_send,
                    recv_sem=ring_recv.at[c, q, m],
                    device_id={"pipe": prv if d == 0 else nxt},
                    device_id_type=MESH,
                ).start()

    def spread_start(c, q, d, t):
        owner = lax.rem(p + t, pipe) if d == 0 else lax.rem(p - t + pipe, pipe)
        m = place(c, d, t)
        pltpu.make_async_remote_copy(
            src_ref=full.at[q, c, owner],
            dst_ref=full.at[q, c, owner],
            send_sem=full_send,
            recv_sem=full_recv.at[c, q, m],
            device_id={"pipe": prv if d == 0 else nxt},
            device_id_type=MESH,
        ).start()

    def spread_wait(c, q, d, t):
        m = place(c, d, t)
        owner = lax.rem(p + t + 1, pipe) if d == 0 else lax.rem(p - t - 1 + pipe, pipe)
        bytes_wait(full.at[q, c, owner], full_recv.at[c, q, m])

    def activate(c):
        sums = []
        for q in range(3):
            value = part[c % 2, q, p]
            for d in range(2):
                m = place(c, d, hops(c, d) - 1)
                bytes_wait(ring_in.at[c, q, m], ring_recv.at[c, q, m])
                value = value + ring_in[c, q, m].astype(F32)
            sums.append(value)
            if q == 1:
                gate, up = sums
                sig = jax.nn.sigmoid(gate)
                full[0, c, p] = (gate * sig * up).astype(BF16)
                for d in range(2):
                    spread_start(c, 0, d, 0)
        gate, up, dh = sums
        full[1, c, p] = (dh * up * sig * (1.0 + gate * (1.0 - sig))).astype(BF16)
        for d in range(2):
            spread_start(c, 1, d, 0)
        full[2, c, p] = (dh * gate * sig).astype(BF16)
        for d in range(2):
            spread_start(c, 2, d, 0)

    def spread_step(c, t):
        for q in range(3):
            for d in range(2):
                if t < hops(c, d):
                    spread_wait(c, q, d, t - 1)
                    spread_start(c, q, d, t)

    def spread_end(c, q):
        for d in range(2):
            spread_wait(c, q, d, hops(c, d) - 1)

    def joined(q, c):
        return jnp.concatenate([full[q, c, i] for i in range(pipe)], axis=1)

    def send_back(c, buf, ret, i):
        to_y = lax.rem(y + rel[c], dp)
        for k in range(ex):
            to_e = lax.rem(e + k, ex)
            if rel[c] == 0 and k == 0:
                copy = pltpu.make_async_copy(buf.at[c, e], ret.at[me], self_sem.at[2 + i])
                copy.start()
                own_copies.append(copy)
                continue
            pltpu.make_async_remote_copy(
                src_ref=buf.at[c, to_e],
                dst_ref=ret.at[me],
                send_sem=send_ret,
                recv_sem=recv_ret.at[i],
                device_id={"dp": to_y, "expert": to_e},
                device_id_type=MESH,
            ).start()

    wtile = 256 if width % 256 == 0 else width

    def expert_out(c):
        h = joined(0, c)
        for n in range(width // wtile):
            cols = slice(n * wtile, (n + 1) * wtile)
            eo_buf[c, :, :, cols] = dot(h, wd[:, cols]).astype(BF16).reshape(ex, CAP, wtile)
        send_back(c, eo_buf, ret_e, 0)

    def input_grad(c):
        dg = joined(1, c)
        du = joined(2, c)
        for n in range(width // wtile):
            cols = slice(n * wtile, (n + 1) * wtile)
            res = dot(dg, wg[cols, :], NT) + dot(du, wu[cols, :], NT)
            dr_buf[c, :, :, cols] = res.astype(BF16).reshape(ex, CAP, wtile)
        send_back(c, dr_buf, ret_d, 1)

    stores = []

    def keep(acc, out, index, c, res):
        if c > 0:
            res = res + acc[index]
        if c == dp - 1:
            out[index] = res.astype(BF16)
        else:
            acc[index] = res

    def gate_grads(c):
        xt = x_of(c).T
        for q, acc, out in ((1, acc_g, grad_g), (2, acc_u, grad_u)):
            for n in range(ff // tile):
                per = tile // fw
                b = jnp.concatenate([full[q, c, n * per + i] for i in range(per)], axis=1)
                keep(acc, out, (slice(None), slice(n * tile, (n + 1) * tile)), c, dot(xt, b))

    def down_grad(c):
        g = g_of(c)
        for i in range(pipe):
            ht = full[0, c, i].T
            keep(acc_d, grad_d, (slice(i * fw, (i + 1) * fw), slice(None)), c, dot(ht, g))

    arrive(0, rows_x, recv_x, own_copies[0])
    loads[0].wait()
    loads[1].wait()
    partial(0, 0)
    partial(0, 1)
    arrive(0, rows_g, recv_g, own_copies[1])
    loads[2].wait()
    partial(0, 2)
    for period in range(dp + 1):
        for t in range(half):
            if period < dp:
                ring_step(period, t)
            if period >= 1:
                if t == 0:
                    activate(period - 1)
                else:
                    spread_step(period - 1, t)
            if t == 0 and period >= 2:
                for q in range(3):
                    spread_end(period - 2, q)
            if period + 1 < dp:
                if t == 0:
                    arrive(period + 1, rows_x, recv_x, None)
                    partial(period + 1, 0)
                elif t == 1:
                    partial(period + 1, 1)
                elif t == 2:
                    arrive(period + 1, rows_g, recv_g, None)
                    partial(period + 1, 2)
            if period >= 2:
                if t == 0:
                    expert_out(period - 2)
                elif t == 1:
                    input_grad(period - 2)
                elif t == 2:
                    gate_grads(period - 2)
                else:
                    down_grad(period - 2)
    last = dp - 1
    spread_end(last, 0)
    expert_out(last)
    spread_end(last, 1)
    spread_end(last, 2)
    input_grad(last)
    gate_grads(last)
    down_grad(last)
    for i, (src, dst) in enumerate(((grad_g, gg_hbm), (grad_u, gu_hbm), (grad_d, gd_hbm))):
        copy = pltpu.make_async_copy(src, dst, store_sem.at[i])
        copy.start()
        stores.append(copy)

    own_copies[2].wait()
    bytes_wait(ret_e.at[pl.ds(0, groups - 1)], recv_ret.at[0])
    back = ret_e[...].reshape(groups * CAP, width)
    mixed_ref[...] = (dot(mix_hi[...], back) + dot(mix_lo[...], back)).astype(BF16)
    own_copies[3].wait()
    bytes_wait(ret_d.at[pl.ds(0, groups - 1)], recv_ret.at[1])
    back = ret_d[...].reshape(groups * CAP, width)
    gtok_ref[...] = dot(onehot_t[...], back).astype(BF16)

    for _ in range(2):
        bytes_wait(out_x.at[pl.ds(0, groups - 1)], send_a2a)
        bytes_wait(out_x.at[pl.ds(0, groups - 1)], send_ret)
    bytes_wait(ring_out, ring_send)
    bytes_wait(ring_out, full_send)
    for copy in stores:
        copy.wait()


def local(sizes, tokens, routes, gates, w_gate, w_up, w_down, grad_out):
    dp, ex, pipe = sizes
    toks, width = tokens.shape
    ff = w_gate.shape[2]
    groups, rows, fw = dp * ex, ex * CAP, ff // pipe
    vmem = pl.BlockSpec(memory_space=pltpu.VMEM)
    hbm = pl.BlockSpec(memory_space=pl.ANY)
    dma = pltpu.SemaphoreType.DMA
    messages = pipe - 1
    mixed, grad_tokens, grad_gate, grad_up, grad_down = pl.pallas_call(
        functools.partial(kernel, dp, ex, pipe),
        out_shape=(
            jax.ShapeDtypeStruct((toks, width), BF16),
            jax.ShapeDtypeStruct((toks, width), BF16),
            jax.ShapeDtypeStruct((width, ff), BF16),
            jax.ShapeDtypeStruct((width, ff), BF16),
            jax.ShapeDtypeStruct((ff, width), BF16),
        ),
        in_specs=[vmem, vmem, vmem, vmem, hbm, hbm, hbm],
        out_specs=(vmem, vmem, hbm, hbm, hbm),
        scratch_shapes=[
            pltpu.VMEM((width, ff), BF16),
            pltpu.VMEM((width, ff), BF16),
            pltpu.VMEM((ff, width), BF16),
            pltpu.VMEM((groups * CAP, toks), F32),
            pltpu.VMEM((groups * CAP, toks), F32),
            pltpu.VMEM((toks, groups * CAP), BF16),
            pltpu.VMEM((toks, groups * CAP), BF16),
            pltpu.VMEM((toks, groups * CAP), BF16),
            pltpu.VMEM((groups, CAP, width), BF16),
            pltpu.VMEM((groups, CAP, width), BF16),
            pltpu.VMEM((dp, ex, CAP, width), BF16),
            pltpu.VMEM((dp, ex, CAP, width), BF16),
            pltpu.VMEM((2, 3, pipe, rows, fw), F32),
            pltpu.VMEM((dp, 3, messages, rows, fw), BF16),
            pltpu.VMEM((dp, 3, messages, rows, fw), BF16),
            pltpu.VMEM((3, dp, pipe, rows, fw), BF16),
            pltpu.VMEM((width, ff), F32),
            pltpu.VMEM((width, ff), F32),
            pltpu.VMEM((ff, width), F32),
            pltpu.VMEM((width, ff), BF16),
            pltpu.VMEM((width, ff), BF16),
            pltpu.VMEM((ff, width), BF16),
            pltpu.VMEM((dp, ex, CAP, width), BF16),
            pltpu.VMEM((dp, ex, CAP, width), BF16),
            pltpu.VMEM((groups, CAP, width), BF16),
            pltpu.VMEM((groups, CAP, width), BF16),
            dma((3,)),
            dma((4,)),
            dma,
            dma((dp,)),
            dma((dp,)),
            dma,
            dma((2,)),
            dma,
            dma((dp, 3, messages)),
            dma,
            dma((dp, 3, messages)),
            dma((3,)),
        ],
        compiler_params=pltpu.CompilerParams(
            collective_id=0, has_side_effects=True, vmem_limit_bytes=60 * 1024 * 1024
        ),
    )(
        routes.T, gates.T, tokens, grad_out,
        w_gate.reshape(width, ff), w_up.reshape(width, ff), w_down.reshape(ff, width),
    )
    return (
        mixed,
        grad_tokens,
        grad_gate.reshape(1, width, ff),
        grad_up.reshape(1, width, ff),
        grad_down.reshape(1, ff, width),
    )


def solution(mesh):
    both = ("dp", "expert")
    sizes = (mesh.shape["dp"], mesh.shape["expert"], mesh.shape["pipe"])
    return jax.shard_map(
        functools.partial(local, sizes),
        mesh=mesh,
        in_specs=(
            P(both, "pipe"),
            P(both, None),
            P(both, None),
            P(both, "pipe", None),
            P(both, "pipe", None),
            P(both, None, "pipe"),
            P(both, "pipe"),
        ),
        out_specs=(
            P(both, "pipe"),
            P(both, "pipe"),
            P(both, "pipe", None),
            P(both, "pipe", None),
            P(both, None, "pipe"),
        ),
        check_vma=False,
    )
```

time: 396 us -> 167 us (0.42)
  waiting for transfers between devices: 264 us -> 0 us
  Pallas kernels: 0 us -> 159 us
  blocking collectives: 46.3 us -> 0 us
  matrix products: 39.7 us -> 0 us
  starting transfers between devices: 22.7 us -> 0 us
  between operations: 14.2 us -> 0.65 us
  other arithmetic: 5.89 us -> 0 us
  local copies, waits for them, and re-layouts: 3.19 us -> 7.19 us
    pallas_call x0 -> x1, Pallas kernels: none -> 159 us  [local(): pl.pallas_call(functools.partial(kernel, dp, ex, pipe), out_shape=(jax.Sh...]
    reduce_scatter x3 -> x0, waiting for transfers between devices: 136 us -> none  [the longest x1 56.5 us: local(): lax.psum_scatter(d_hidden_part, 'pipe', scatter_dimension=3, tiled=True)]
    all_gather x3 -> x0, waiting for transfers between devices: 116 us -> none  [the longest x1 41.7 us: local(): lax.all_gather(d_gate_share, 'pipe', axis=3, tiled=True)]
    all_to_all x2 -> x0, blocking collectives: 46.3 us -> none  [the longest x1 25.6 us: local(): lax.all_to_all(outbound, ('dp', 'expert'), split_axis=0, concat_axis=0, t...]
    dot_general x13 -> x0, matrix products: 39.7 us -> none  [the longest x1 4.95 us: local(): jnp.einsum('sjcf,jdf->sjcd', d_gate, w_gate, preferred_element_type=jnp.f...]
    all_to_all x2 -> x0, starting transfers between devices: 22.5 us -> none  [the longest x1 11.2 us: local(): lax.all_to_all(expert_out.reshape(num_experts, CAP, slice_width), ('dp',...]
    all_to_all x2 -> x0, waiting for transfers between devices: 10.8 us -> none  [the longest x1 10.8 us: local(): lax.all_to_all(d_rows.reshape(num_experts, CAP, slice_width), ('dp', 'exp...]
    unnamed x17 -> x11, local copies, waits for them, and re-layouts: 2.48 us -> 7.19 us
  transfers between devices with their start and end apart: 8 -> 0, of which waited for: 7 -> 0; matrix products, arithmetic and copies ran while one was open for 8% -> 0% of each run, Pallas kernels for 0% -> 0%
where the time goes in v1:
time: 167 us
  Pallas kernels  159 us (95%)
  local copies, waits for them, and re-layouts  7.19 us (4%)
    pallas_call x1, Pallas kernels, local(): pl.pallas_call(functools.partial(kernel, dp, ex, pipe), out_shape=(jax.Sh...  159 us
    unnamed x11, local copies, waits for them, and re-layouts  7.19 us

profile of v1, /device:TPU:1, one launch (start us, length us, event | category | flops | bytes accessed | tf_op | source)
XLA Modules:
  0.0 166.8 jit_solution(907365900111949140)
XLA Ops:
  0.6 159.0 %shard_map.110 = (bf16[128,512]{1,0:T(8,128)(2,1)}, bf16[128,512]{1,0:T(8,128)(2,1)}, bf16[512,1024]{1,0:T(8,128)(2,1)}, bf16[512,1024]{1,0:T(8,128)(2,1)}, bf16[1024,512]{1,0:T(8,128)(2,1)}) custom-call(s32[6,128]{1,0:T(8,128)} %bitcast.14, f32[6,128]{1,0:T(8,128)} %bitcast.15, bf16[128,512]{1,0:T(8,128)(2,1)} %tok_ref.1, bf16[128,512]{1,0:T(8,128)(2,1)} %go_ref.1, ...), custom_call_target="tpu_custom_call" | custom-call | tf_op jit(solution)/shard_map/pallas_call | solution.py:383
  159.6 0.0 copy-start.2
  159.7 1.6 copy.17
  161.3 0.0 copy-done.2
  161.3 0.7 copy.18
  161.9 0.0 copy-start.1
  161.9 2.4 %copy.19 = bf16[1,512,1024]{2,1,0:T(8,128)(2,1)} copy(bf16[1,512,1024]{2,1,0:T(8,128)(2,1)} %bitcast.13) | data formatting | bytes 2097152
  164.3 0.0 copy-done.1
  164.3 0.0 copy-start
  164.3 1.0 copy.20
  165.2 0.6 copy-done
  165.9 1.0 copy.21
Async XLA Ops:
  159.6 1.6 copy-start.2
  161.9 2.4 %copy-start.1 = (bf16[512,1024]{1,0:T(8,128)(2,1)S(1)}, bf16[512,1024]{1,0:T(8,128)(2,1)}, u32[]{:S(2)}) copy-start(bf16[512,1024]{1,0:T(8,128)(2,1)} %get-tuple-element.13) | copy-start | bytes 3145732
  164.3 1.6 copy-start

commit v2 on v1

--- a/solution.py
+++ b/solution.py
@@ -20,7 +20,7 @@
 
 
 def chunk_order(dp):
-    return {4: (0, 2, 1, 3), 2: (0, 1), 1: (0,)}[dp]
+    return {4: (0, 1, 2, 3), 2: (0, 1), 1: (0,)}[dp]
 
 
 def kernel(
@@ -101,7 +101,8 @@
     pl.semaphore_wait(barrier, groups - 1 + 2)
 
     own_copies = []
-    for c in range(dp):
+
+    def dispatch(c):
         to_y = lax.rem(y - rel[c] + dp, dp)
         for src, dst, recv in ((out_x, rows_x, recv_x), (out_g, rows_g, recv_g)):
             for k in range(ex):
@@ -121,6 +122,9 @@
                     device_id={"dp": to_y, "expert": to_e},
                     device_id_type=MESH,
                 ).start()
+
+    for c in range(min(dp, 2)):
+        dispatch(c)
 
     onehot_t[...] = onehot[...].T.astype(BF16)
     mix_t = mixw[...].T
@@ -314,6 +318,9 @@
         for t in range(half):
             if period < dp:
                 ring_step(period, t)
+            if period == 0 and t == 0:
+                for c in range(2, dp):
+                    dispatch(c)
             if period >= 1:
                 if t == 0:
                     activate(period - 1)
@@ -323,12 +330,13 @@
                 for q in range(3):
                     spread_end(period - 2, q)
             if period + 1 < dp:
-                if t == 0:
+                first = 1 if period == 0 else 0
+                if t == first:
                     arrive(period + 1, rows_x, recv_x, None)
                     partial(period + 1, 0)
-                elif t == 1:
+                elif t == first + 1:
                     partial(period + 1, 1)
-                elif t == 2:
+                elif t == first + 2:
                     arrive(period + 1, rows_g, recv_g, None)
                     partial(period + 1, 2)
             if period >= 2:
@@ -343,15 +351,20 @@
     last = dp - 1
     spread_end(last, 0)
     expert_out(last)
+    down_grad(last)
+
+    def store(i, src, dst):
+        copy = pltpu.make_async_copy(src, dst, store_sem.at[i])
+        copy.start()
+        stores.append(copy)
+
+    store(2, grad_d, gd_hbm)
     spread_end(last, 1)
     spread_end(last, 2)
     input_grad(last)
     gate_grads(last)
-    down_grad(last)
-    for i, (src, dst) in enumerate(((grad_g, gg_hbm), (grad_u, gu_hbm), (grad_d, gd_hbm))):
-        copy = pltpu.make_async_copy(src, dst, store_sem.at[i])
-        copy.start()
-        stores.append(copy)
+    store(0, grad_g, gg_hbm)
+    store(1, grad_u, gu_hbm)
 
     own_copies[2].wait()
     bytes_wait(ret_e.at[pl.ds(0, groups - 1)], recv_ret.at[0])
@@ -368,6 +381,20 @@
     bytes_wait(ring_out, ring_send)
     bytes_wait(ring_out, full_send)
     for copy in stores:
+        copy.wait()
+
+
+def hand_out(count, *refs):
+    src, dst, buf = (refs[i * count : (i + 1) * count] for i in range(3))
+    in_sem, out_sem = refs[3 * count :]
+    ins = [pltpu.make_async_copy(src[i], buf[i], in_sem.at[i]) for i in range(count)]
+    outs = [pltpu.make_async_copy(buf[i], dst[i], out_sem.at[i]) for i in range(count)]
+    for copy in ins:
+        copy.start()
+    for i in range(count):
+        ins[i].wait()
+        outs[i].start()
+    for copy in outs:
         copy.wait()
 
 
@@ -380,7 +407,7 @@
     hbm = pl.BlockSpec(memory_space=pl.ANY)
     dma = pltpu.SemaphoreType.DMA
     messages = pipe - 1
-    mixed, grad_tokens, grad_gate, grad_up, grad_down = pl.pallas_call(
+    results = pl.pallas_call(
         functools.partial(kernel, dp, ex, pipe),
         out_shape=(
             jax.ShapeDtypeStruct((toks, width), BF16),
@@ -438,6 +465,15 @@
         routes.T, gates.T, tokens, grad_out,
         w_gate.reshape(width, ff), w_up.reshape(width, ff), w_down.reshape(ff, width),
     )
+    count = len(results)
+    mixed, grad_tokens, grad_gate, grad_up, grad_down = pl.pallas_call(
+        functools.partial(hand_out, count),
+        out_shape=tuple(jax.ShapeDtypeStruct(r.shape, r.dtype) for r in results),
+        in_specs=[hbm] * count,
+        out_specs=(hbm,) * count,
+        scratch_shapes=[pltpu.VMEM(r.shape, r.dtype) for r in results] + [dma((count,))] * 2,
+        compiler_params=pltpu.CompilerParams(vmem_limit_bytes=60 * 1024 * 1024),
+    )(*results)
     return (
         mixed,
         grad_tokens,

time: 167 us -> 161 us (0.964)
  local copies, waits for them, and re-layouts: 7.19 us -> 0 us
    unnamed x11 -> x0, local copies, waits for them, and re-layouts: 7.19 us -> none
    pallas_call x0 -> x1, Pallas kernels: none -> 3.15 us  [local(): pl.pallas_call(functools.partial(hand_out, count), out_shape=tuple((jax.S...]
    pallas_call x1, Pallas kernels: 159 us -> 157 us  [local(): pl.pallas_call(functools.partial(kernel, dp, ex, pipe), out_shape=(jax.Sh...]
where the time goes in v2:
time: 161 us
  Pallas kernels  160 us (99%)
    pallas_call x1, Pallas kernels, local(): pl.pallas_call(functools.partial(kernel, dp, ex, pipe), out_shape=(jax.Sh...  157 us

profile of v2, /device:TPU:1, one launch (start us, length us, event | category | flops | bytes accessed | tf_op | source)
XLA Modules:
  0.0 161.0 jit_solution(17483850405081820766)
XLA Ops:
  0.6 157.1 %shard_map.110 = (bf16[128,512]{1,0:T(8,128)(2,1)}, bf16[128,512]{1,0:T(8,128)(2,1)}, bf16[512,1024]{1,0:T(8,128)(2,1)}, bf16[512,1024]{1,0:T(8,128)(2,1)}, bf16[1024,512]{1,0:T(8,128)(2,1)}) custom-call(s32[6,128]{1,0:T(8,128)} %bitcast.11, f32[6,128]{1,0:T(8,128)} %bitcast.12, bf16[128,512]{1,0:T(8,128)(2,1)} %tok_ref.1, bf16[128,512]{1,0:T(8,128)(2,1)} %go_ref.1, ...), custom_call_target="tpu_custom_call" | custom-call | tf_op jit(solution)/shard_map/pallas_call | solution.py:410
  157.7 3.2 %shard_map.111 = (bf16[128,512]{1,0:T(8,128)(2,1)}, bf16[128,512]{1,0:T(8,128)(2,1)}, bf16[512,1024]{1,0:T(8,128)(2,1)}, bf16[512,1024]{1,0:T(8,128)(2,1)}, bf16[1024,512]{1,0:T(8,128)(2,1)}) custom-call(bf16[128,512]{1,0:T(8,128)(2,1)} %get-tuple-element.15.refs_0_, bf16[128,512]{1,0:T(8,128)(2,1)} %get-tuple-element.16.refs_1_, ...), custom_call_target="tpu_custom_call" | custom-call | tf_op jit(solution)/shard_map/pallas_call | solution.py:469
